TPU v7x, 512 devices: a whole 4x4x16 slice. The times are simulated.
512 devices in a mesh: section: 16 (over z), expert: 8 (over y, core), dp: 4 (over x).
Axes of the slice: x: 4, y: 4, z: 16, core: 2. Of those that a mesh axis runs over, the one named last changes fastest.
Arguments:
- tokens: bfloat16 [1024, 3072], P('expert', 'dp'), may hold values from -6 to 6
- expert_ids: int32 [1024, 2], P('expert'), may hold values from 0 to 7, all different within a row; in each aligned block of 128 rows (0 to 127, 128 to 255, ...) at most 64 rows name the same one
- w_gate: bfloat16 [8, 3072, 8192], P('expert', 'dp', 'section'), may hold values from -0.109375 to 0.109375
- w_up: bfloat16 [8, 3072, 8192], P('expert', 'dp', 'section'), may hold values from -0.109375 to 0.109375
- cotangent: bfloat16 [8, 512, 8192], P('expert', None, 'section'), may hold values from -6 to 6
Outputs:
- acted: bfloat16 [8, 512, 8192], P('expert', None, 'section')
- input_grad: bfloat16 [1024, 3072], P('expert', 'dp')
- gate_grad: bfloat16 [8, 3072, 8192], P('expert', 'dp', 'section')
- up_grad: bfloat16 [8, 3072, 8192], P('expert', 'dp', 'section')
Inputs may be any that keep to these rules, and one draw needn't show every extreme that they name: `expert_ids`: each token names two different experts. Among the 128 tokens of one index of the expert axis no expert is named more than 64 times, a bound that some block reaches.
All inputs are finite; a program needn't handle non-finite values.
Results may differ from a plain program's by a relative error of at most 0.0049.
Values may be sent and summed in bfloat16 or wider, within the bound.
A program may use at most 64 MiB of HBM per device.

v0:
```python
import jax
import jax.numpy as jnp
from jax import lax
from jax.sharding import PartitionSpec as P


def local(tokens, expert_ids, w_gate, w_up, cotangent):
    rows, width = tokens.shape
    experts = lax.axis_size("expert")
    capacity = min(rows, 4 * rows // experts)
    wg = w_gate[0]
    wu = w_up[0]
    flat_ids = expert_ids.reshape(-1)
    member = (flat_ids[:, None] == jnp.arange(experts, dtype=jnp.int32)[None, :]).astype(jnp.int32)
    rank = jnp.sum((jnp.cumsum(member, axis=0) - member) * member, axis=1)
    slot = flat_ids * capacity + rank
    token_of = jnp.arange(2 * rows, dtype=jnp.int32) // 2
    source = jnp.full((experts * capacity,), rows, jnp.int32).at[slot].set(token_of)
    occupied = jnp.zeros((experts * capacity,), jnp.bfloat16).at[slot].set(1.0)
    x_pad = jnp.concatenate([tokens, jnp.zeros((1, width), jnp.bfloat16)], axis=0)
    send_x = jnp.take(x_pad, source, axis=0).reshape(experts, capacity, width)
    recv_x, recv_live = (
        lax.all_to_all(send_x, "expert", split_axis=0, concat_axis=0, tiled=True),
        lax.all_to_all(
            occupied.reshape(experts, capacity), "expert", split_axis=0, concat_axis=0, tiled=True
        ),
    )
    x_rows = recv_x.reshape(-1, width)
    parts = (x_rows,)
    part_gate = jnp.dot(parts[0], wg, preferred_element_type=jnp.float32)
    part_up = jnp.dot(parts[0], wu, preferred_element_type=jnp.float32)
    pre_gate, pre_up = lax.psum((part_gate, part_up), "dp")
    sig = jax.nn.sigmoid(pre_gate)
    silu_v = pre_gate * sig
    acted = (silu_v * pre_up).astype(jnp.bfloat16)
    cf = cotangent[0].astype(jnp.float32)
    gate_part = (cf * pre_up * sig * (1.0 + pre_gate * (1.0 - sig))).astype(jnp.bfloat16)
    up_part = (cf * silu_v).astype(jnp.bfloat16)
    contract = (((0,), (0,)), ((), ()))
    gate_grad = lax.dot_general(x_rows, gate_part, contract, preferred_element_type=jnp.float32)
    up_grad = lax.dot_general(x_rows, up_part, contract, preferred_element_type=jnp.float32)
    parts = (gate_part, up_part)
    back = lax.dot_general(
        parts[0], wg, (((1,), (1,)), ((), ())), preferred_element_type=jnp.float32
    ) + lax.dot_general(parts[1], wu, (((1,), (1,)), ((), ())), preferred_element_type=jnp.float32)
    back = (back,)[0]
    whole = lax.psum(back, "section")
    home = lax.all_to_all(
        whole.reshape(experts, capacity, width), "expert", split_axis=0, concat_axis=0, tiled=True
    )
    token_grad = jnp.sum(
        jnp.take(home.reshape(-1, width), slot, axis=0).reshape(rows, 2, width), axis=1
    )
    return (
        acted[None],
        token_grad.astype(jnp.bfloat16),
        gate_grad.astype(jnp.bfloat16)[None],
        up_grad.astype(jnp.bfloat16)[None],
    )


def solution(mesh):
    placed = (
        P("expert", "dp"),
        P("expert", None),
        P("expert", "dp", "section"),
        P("expert", "dp", "section"),
        P("expert", None, "section"),
    )
    return jax.shard_map(
        local,
        mesh=mesh,
        in_specs=placed,
        out_specs=(
            P("expert", None, "section"),
            P("expert", "dp"),
            P("expert", "dp", "section"),
            P("expert", "dp", "section"),
        ),
        check_vma=False,
    )
```

profile of v0, /device:TPU:24, one launch (start us, length us, event | category | flops | bytes accessed | tf_op | source)
XLA Modules:
  0.0 294.9 jit_solution(851770255115678732)
XLA Ops:
  7.2 0.0 copy-start
  7.2 0.0 all-reduce.7.cloned.1.call-start
  7.2 0.7 broadcast_multiply_fusion
  8.0 0.8 copy.14
  8.8 0.1 eq.29
  8.9 0.1 eq.25
  9.0 0.1 copy.13
  9.2 0.1 mul.45
  9.3 0.6 reduce-window.6
  9.9 0.2 slice_reduce_fusion
  10.2 0.1 fusion.16
  10.3 1.4 scatter_custom_fusion
  11.7 0.1 broadcast_in_dim.40
  11.8 0.9 concatenate.3
  12.7 2.0 gather_fusion
  14.8 0.0 copy-start.4
  14.8 0.1 broadcast_select_fusion
  14.9 19.2 %all_to_all.10 = bf16[8,64,768]{2,1,0:T(8,128)(2,1)S(1)} all-to-all(bf16[8,64,768]{2,1,0:T(8,128)(2,1)S(1)} %broadcast_select_fusion), channel_id=1, replica_groups=mesh['section'=16,'expert'=8,'dp'=4] {'expert'}, dimensions={0} | all-to-all | bytes 1572864 | tf_op jit(solution)/shard_map/all_to_all | solution.py:23
  34.1 0.0 copy-done.4
  34.1 1.6 fusion.8
  35.7 0.0 copy-done
  35.7 1.6 fusion.12
  37.3 0.0 copy-start.6
  37.3 0.0 all-reduce.7.cloned.1.call-update
  37.3 0.0 all-reduce.5.cloned.1.call-start
  37.4 74.7 %all-reduce.7.cloned.1.call-done = (f32[512,512]{1,0:T(8,128)}, f32[512,512]{1,0:T(8,128)}) async-done(((f32[512,512]{1,0:T(8,128)}, f32[512,512]{1,0:T(8,128)}), (f32[512,512]{1,0:T(8,128)}, f32[512,512]{1,0:T(8,128)})) %all-reduce.7.cloned.1.call-update) | async-done | bytes 2097168 | tf_op jit(solution)/shard_map/psum | solution.py:32
  112.1 0.0 copy-done.6
  112.1 2.9 fusion.4
  115.0 0.0 copy-start.1
  115.0 0.0 copy-start.2
  115.0 0.0 copy-start.5
  115.0 0.0 copy-start.7
  115.0 0.6 fusion.10
  115.6 0.8 copy-done.2
  116.4 0.2 copy-done.5
  116.6 0.1 copy-done.7
  116.8 1.9 convolution_add_fusion
  118.7 0.0 copy-done.1
  118.7 0.0 all-reduce.5.cloned.1.call-update
  118.7 0.0 copy-start.9
  118.7 141.7 %all-reduce.5.cloned.1.call-done = f32[8,64,768]{2,1,0:T(8,128)} async-done(((f32[8,64,768]{2,1,0:T(8,128)}), f32[8,64,768]{2,1,0:T(8,128)}) %all-reduce.5.cloned.1.call-update) | async-done | bytes 1572880 | tf_op jit(solution)/shard_map/psum | solution.py:47
  260.5 4.8 %all-to-all-start.1 = ((f32[8,64,768]{2,1,0:T(8,128)}), f32[8,64,768]{2,1,0:T(8,128)S(1)}, u32[]{:S(2)}, u32[]{:S(2)}) async-start(f32[8,64,768]{2,1,0:T(8,128)} %all-reduce.5.cloned.1.call-done), calls=%async_computation.1 | async-start | bytes 3145728 | tf_op jit(solution)/shard_map/all_to_all | solution.py:48
  265.2 0.1 reduce_sum.24
  265.4 0.1 copy.16
  265.4 0.0 copy-done.9
  265.5 0.1 copy.17
  265.6 0.0 copy-start.3
  265.6 0.0 copy-start.8
  265.7 2.6 fusion
  268.3 0.0 copy-done.3
  268.3 0.0 copy-done.8
  268.3 1.6 fusion.1
  269.9 14.8 %all-to-all-done.1 = f32[8,64,768]{2,1,0:T(8,128)S(1)} async-done(((f32[8,64,768]{2,1,0:T(8,128)}), f32[8,64,768]{2,1,0:T(8,128)S(1)}, u32[]{:S(2)}, u32[]{:S(2)}) %all-to-all-start.1) | async-done | bytes 1572896 | tf_op jit(solution)/shard_map/all_to_all | solution.py:48
  284.7 1.1 gather_fusion.1
  285.8 0.5 gather.15
  286.3 1.8 select_reduce_fusion
  (10 shorter events, 0.1 us)
Async XLA Ops:
  7.2 28.6 %copy-start = (bf16[1,768,512]{2,1,0:T(8,128)(2,1)S(1)}, bf16[1,768,512]{2,1,0:T(8,128)(2,1)}, u32[]{:S(2)}) copy-start(bf16[1,768,512]{2,1,0:T(8,128)(2,1)} %param.7) | copy-start | bytes 2359300
  7.2 104.9 %all-reduce.7.cloned.1.call-start = ((), (), s32[]{:S(2)}) async-start(), calls=%async_computation.3 | async-start | bytes 4194304 | tf_op jit(solution)/shard_map/psum | solution.py:32
  14.8 19.4 %copy-start.4 = (bf16[1,768,512]{2,1,0:T(8,128)(2,1)S(1)}, bf16[1,768,512]{2,1,0:T(8,128)(2,1)}, u32[]{:S(2)}) copy-start(bf16[1,768,512]{2,1,0:T(8,128)(2,1)} %param.8) | copy-start | bytes 2359300
  37.3 74.8 %copy-start.6 = (bf16[1,512,512]{2,1,0:T(8,128)(2,1)S(1)}, bf16[1,512,512]{2,1,0:T(8,128)(2,1)}, u32[]{:S(2)}) copy-start(bf16[1,512,512]{2,1,0:T(8,128)(2,1)} %param.9) | copy-start | bytes 1572868
  37.3 223.1 %all-reduce.5.cloned.1.call-start = ((), (), s32[]{:S(2)}) async-start(), calls=%async_computation.2 | async-start | bytes 3145728 | tf_op jit(solution)/shard_map/psum | solution.py:47
  115.0 3.7 %copy-start.1 = (bf16[512,512]{1,0:T(8,128)(2,1)}, bf16[512,512]{1,0:T(8,128)(2,1)S(1)}, u32[]{:S(2)}) copy-start(bf16[512,512]{1,0:T(8,128)(2,1)S(1)} %get-tuple-element.6) | copy-start | bytes 1572868
  115.0 1.4 copy-start.2
  115.0 1.6 copy-start.5
  115.0 1.8 copy-start.7
  118.7 146.7 %copy-start.9 = (s32[128,2]{0,1:T(2,128)S(1)}, s32[128,2]{0,1:T(2,128)}, u32[]{:S(2)}) copy-start(s32[128,2]{0,1:T(2,128)} %param.6) | copy-start | bytes 3076
  260.5 24.3 %all-to-all-start.1 = ((f32[8,64,768]{2,1,0:T(8,128)}), f32[8,64,768]{2,1,0:T(8,128)S(1)}, u32[]{:S(2)}, u32[]{:S(2)}) async-start(f32[8,64,768]{2,1,0:T(8,128)} %all-reduce.5.cloned.1.call-done), calls=%async_computation.1 | async-start | bytes 3145728 | tf_op jit(solution)/shard_map/all_to_all | solution.py:48
  265.6 2.7 copy-start.3
  265.6 2.7 copy-start.8
Sparse Core Ops, SparseCore 0:
  37.5 74.5 all-reduce.6
  118.8 141.5 all-reduce.4
where the time goes:
time: 298 us; the launch traced here: 295 us
  waiting for transfers between devices  231 us (78%)
  blocking collectives  19.2 us (6%)
  between operations  14.2 us (5%)
  matrix products  9.94 us (3%)
  local copies, waits for them, and re-layouts  9.07 us (3%)
  other arithmetic  6.29 us (2%)
  starting transfers between devices  4.86 us (2%)
    psum x1, waiting for transfers between devices, local(): whole = lax.psum(back, 'section')  142 us
    psum x1, waiting for transfers between devices, local(): pre_gate, pre_up = lax.psum((part_gate, part_up), 'dp')  74.7 us
    all_to_all x1, blocking collectives, local(): lax.all_to_all(send_x, 'expert', split_axis=0, concat_axis=0, tiled=True)  19.2 us
    all_to_all x1, waiting for transfers between devices, local(): lax.all_to_all(whole.reshape(experts, capacity, width), 'expert', split_a...  14.8 us
  transfers between devices with their start and end apart: 3, of which 3 were waited for; matrix products, arithmetic and copies ran while one was open for 2% of the time, Pallas kernels for 0%

commit v1 on v0

v1 whole, which is shorter than its diff:
```python
import jax
import jax.numpy as jnp
from jax import lax
from jax.experimental import pallas as pl
from jax.experimental.pallas import tpu as pltpu
from jax.sharding import PartitionSpec as P

F32 = jnp.float32
BF16 = jnp.bfloat16
NN = (((1,), (0,)), ((), ()))
NT = (((1,), (1,)), ((), ()))
TN = (((0,), (0,)), ((), ()))


def dot(a, b, dims):
    return lax.dot_general(a, b, dims, preferred_element_type=F32)


def kernel(
    sizes,
    tok, slots, wg, wu, cot,
    acted, grad_in, grad_gate, grad_up,
    pick, x_out, x_all, pre_out, pre_in, pre_own, pre_all,
    gate_part, up_part, back_out, home, whole, z_out, z_in, z_all,
    x_ss, x_rs, p_ss, p_rs, a_ss, a_rs, h_ss, h_rs, zr_ss, zr_rs, za_ss, za_rs,
):
    ns, ne, nd = sizes
    s, e, d = lax.axis_index("section"), lax.axis_index("expert"), lax.axis_index("dp")
    cap = x_all.shape[0] // ne
    hid = wg.shape[1]
    per = ne // nd
    y, c = e // 2, e % 2
    ny = ne // 2

    def rows(g):
        return pl.ds(pl.multiple_of(g * cap, cap), cap)

    def expert_peer(k):
        return ((y + k // 2) % ny) * 2 + (c + k) % 2

    def send(src, dst, ss, rs, axis, peer):
        return pltpu.make_async_remote_copy(
            src_ref=src, dst_ref=dst, send_sem=ss, recv_sem=rs,
            device_id={axis: peer}, device_id_type=pl.DeviceIdType.MESH,
        )

    barrier = pltpu.get_barrier_semaphore()
    for axis, me, n in (("section", s, ns), ("expert", e, ne), ("dp", d, nd)):
        for k in range(1, n):
            pl.semaphore_signal(
                barrier, inc=1, device_id={axis: (me + k) % n},
                device_id_type=pl.DeviceIdType.MESH,
            )

    at = lax.broadcasted_iota(jnp.int32, pick.shape, 0)
    pick[...] = jnp.where(
        (at == slots[0:1, :]) | (at == slots[1:2, :]), 1.0, 0.0
    ).astype(BF16)

    def build(g, _):
        x_out[rows(g), :] = dot(pick[rows(g), :], tok[...], NN).astype(BF16)
        return 0

    lax.fori_loop(0, ne, build, 0)
    x_all[rows(e), :] = x_out[rows(e), :]
    pl.semaphore_wait(barrier, ns + ne + nd - 3)

    def x_copy(peer, slot):
        return send(
            x_out.at[rows(peer)], x_all.at[rows(slot)], x_ss.at[peer], x_rs.at[slot],
            "expert", peer,
        )

    for k in range(1, ne):
        x_copy(expert_peer(k), e).start()

    def p_copy(g):
        i = g // nd
        return send(
            pre_out.at[rows(g)], pre_in.at[i, d], p_ss.at[g], p_rs.at[i, d], "dp", g % nd
        )

    def forward(k, _):
        g = expert_peer(k)

        @pl.when(k > 0)
        def _():
            x_copy(g, g).wait_recv()

        x = x_all[rows(g), :]
        pg = dot(x, wg[...], NN)
        pu = dot(x, wu[...], NN)

        @pl.when(g % nd == d)
        def _():
            pre_own[g // nd, :, :hid] = pg
            pre_own[g // nd, :, hid:] = pu

        @pl.when(g % nd != d)
        def _():
            pre_out[rows(g), :hid] = pg.astype(BF16)
            pre_out[rows(g), hid:] = pu.astype(BF16)
            p_copy(g).start()

        return 0

    lax.fori_loop(0, ne, forward, 0)

    def a_copy(i, peer, g):
        return send(
            pre_all.at[rows(g)], pre_all.at[rows(g)], a_ss.at[i, peer], a_rs.at[g], "dp", peer
        )

    def owned(i, _):
        total = pre_own[i]
        for k in range(1, nd):
            src = (d + k) % nd
            send(
                pre_out.at[rows(0)], pre_in.at[i, src], p_ss.at[0], p_rs.at[i, src], "dp", src
            ).wait_recv()
            total = total + pre_in[i, src].astype(F32)
        g = i * nd + d
        pre_all[rows(g), :] = total.astype(BF16)
        for k in range(1, nd):
            a_copy(i, (d + k) % nd, g).start()
        return 0

    lax.fori_loop(0, per, owned, 0)

    def h_copy(g):
        return send(back_out.at[rows(g)], home.at[rows(e)], h_ss.at[g], h_rs.at[e], "expert", g)

    def backward(t, _):
        i, k = t // nd, t % nd
        src = (d + k) % nd
        g = i * nd + src

        @pl.when(k > 0)
        def _():
            a_copy(i, src, g).wait_recv()

        pre_gate = pre_all[rows(g), :hid].astype(F32)
        pre_up = pre_all[rows(g), hid:].astype(F32)
        cf = cot[rows(g), :].astype(F32)
        sig = jax.nn.sigmoid(pre_gate)
        silu = pre_gate * sig
        acted[rows(g), :] = (silu * pre_up).astype(BF16)
        gp = (cf * pre_up * sig * (1.0 + pre_gate * (1.0 - sig))).astype(BF16)
        up = (cf * silu).astype(BF16)
        gate_part[rows(g), :] = gp
        up_part[rows(g), :] = up
        back = (dot(gp, wg[...], NT) + dot(up, wu[...], NT)).astype(BF16)

        @pl.when(g == e)
        def _():
            home[rows(g), :] = back

        @pl.when(g != e)
        def _():
            back_out[rows(g), :] = back
            h_copy(g).start()

        return 0

    lax.fori_loop(0, ne, backward, 0)

    tile = 128

    def weights(i, _):
        at = pl.ds(pl.multiple_of(i * tile, tile), tile)
        x = x_all[:, at]
        grad_gate[at, :] = dot(x, gate_part[...], TN).astype(BF16)
        grad_up[at, :] = dot(x, up_part[...], TN).astype(BF16)
        return 0

    lax.fori_loop(0, wg.shape[0] // tile, weights, 0)

    for k in range(1, ne):
        src = expert_peer(k)
        send(
            back_out.at[rows(src)], home.at[rows(src)], h_ss.at[src], h_rs.at[src], "expert", src
        ).wait_recv()
    part = dot(pick[...], home[...], TN).reshape(whole.shape)
    whole[...] = part
    z_out[...] = part.astype(BF16)

    far = [k for j in range(ns // 2, 0, -1) for k in dict.fromkeys((j, ns - j))]

    def zr_copy(peer, slot):
        return send(
            z_out.at[peer], z_in.at[slot], zr_ss.at[peer], zr_rs.at[slot], "section", peer
        )

    def za_copy(peer, slot):
        return send(
            z_all.at[slot], z_all.at[slot], za_ss.at[peer], za_rs.at[slot], "section", peer
        )

    for k in far:
        zr_copy((s + k) % ns, s).start()
    total = whole[s]
    for k in reversed(far):
        src = (s + k) % ns
        zr_copy(src, src).wait_recv()
        total = total + z_in[src].astype(F32)
    z_all[s] = total.astype(BF16)
    for k in far:
        za_copy((s + k) % ns, s).start()
    for k in reversed(far):
        src = (s + k) % ns
        za_copy(src, src).wait_recv()
    grad_in[...] = z_all[...]

    for k in range(1, ne):
        x_copy(expert_peer(k), e).wait_send()
        h_copy(expert_peer(k)).wait_send()
    for i in range(per):
        for k in range(1, nd):
            p_copy(i * nd + (d + k) % nd).wait_send()
            a_copy(i, (d + k) % nd, i * nd + d).wait_send()
    for k in far:
        zr_copy((s + k) % ns, s).wait_send()
        za_copy((s + k) % ns, s).wait_send()


def local(tokens, expert_ids, w_gate, w_up, cotangent):
    count, width = tokens.shape
    ns, ne, nd = (lax.axis_size(a) for a in ("section", "expert", "dp"))
    hid = w_gate.shape[2]
    slots = cotangent.shape[1]
    cap = slots // ne
    flat = expert_ids.reshape(-1)
    order = jnp.arange(2 * count, dtype=jnp.int32)
    earlier = (flat[:, None] == flat[None, :]) & (order[None, :] < order[:, None])
    slot = flat * cap + jnp.sum(earlier.astype(jnp.int32), axis=1)
    slot = slot.reshape(count, 2).T

    vmem = pl.BlockSpec(memory_space=pltpu.VMEM)
    dma = pltpu.SemaphoreType.DMA
    share = count // ns
    acted, grad_in, grad_gate, grad_up = pl.pallas_call(
        lambda *refs: kernel((ns, ne, nd), *refs),
        out_shape=(
            jax.ShapeDtypeStruct((slots, hid), BF16),
            jax.ShapeDtypeStruct((ns, share, width), BF16),
            jax.ShapeDtypeStruct((width, hid), BF16),
            jax.ShapeDtypeStruct((width, hid), BF16),
        ),
        in_specs=[vmem] * 5,
        out_specs=(vmem,) * 4,
        scratch_shapes=[
            pltpu.VMEM((slots, count), BF16),
            pltpu.VMEM((slots, width), BF16),
            pltpu.VMEM((slots, width), BF16),
            pltpu.VMEM((slots, 2 * hid), BF16),
            pltpu.VMEM((ne // nd, nd, cap, 2 * hid), BF16),
            pltpu.VMEM((ne // nd, cap, 2 * hid), F32),
            pltpu.VMEM((slots, 2 * hid), BF16),
            pltpu.VMEM((slots, hid), BF16),
            pltpu.VMEM((slots, hid), BF16),
            pltpu.VMEM((slots, width), BF16),
            pltpu.VMEM((slots, width), BF16),
            pltpu.VMEM((ns, share, width), F32),
            pltpu.VMEM((ns, share, width), BF16),
            pltpu.VMEM((ns, share, width), BF16),
            pltpu.VMEM((ns, share, width), BF16),
            dma((ne,)), dma((ne,)),
            dma((ne,)), dma((ne // nd, nd)),
            dma((ne // nd, nd)), dma((ne,)),
            dma((ne,)), dma((ne,)),
            dma((ns,)), dma((ns,)),
            dma((ns,)), dma((ns,)),
        ],
        compiler_params=pltpu.CompilerParams(collective_id=0, has_side_effects=True),
    )(tokens, slot, w_gate[0], w_up[0], cotangent[0])
    return acted[None], grad_in.reshape(count, width), grad_gate[None], grad_up[None]


def solution(mesh):
    placed = (
        P("expert", "dp"),
        P("expert", None),
        P("expert", "dp", "section"),
        P("expert", "dp", "section"),
        P("expert", None, "section"),
    )
    return jax.shard_map(
        local,
        mesh=mesh,
        in_specs=placed,
        out_specs=(
            P("expert", None, "section"),
            P("expert", "dp"),
            P("expert", "dp", "section"),
            P("expert", "dp", "section"),
        ),
        check_vma=False,
    )
```

time: 298 us -> 92.3 us (0.31)
  waiting for transfers between devices: 231 us -> 0 us
  Pallas kernels: 0 us -> 84.5 us
  blocking collectives: 19.2 us -> 0 us
  between operations: 14.2 us -> 0.68 us
  matrix products: 9.94 us -> 0 us
  other arithmetic: 6.29 us -> 0.78 us
  starting transfers between devices: 4.86 us -> 0 us
  local copies, waits for them, and re-layouts: 9.07 us -> 6.07 us
    psum x2 -> x0, waiting for transfers between devices: 216 us -> none  [the longest x1 142 us: local(): whole = lax.psum(back, 'section')]
    pallas_call x0 -> x1, Pallas kernels: none -> 84.5 us  [local(): pl.pallas_call(lambda *refs: kernel((ns, ne, nd), *refs), out_shape=(jax....]
    all_to_all x1 -> x0, blocking collectives: 19.2 us -> none  [local(): lax.all_to_all(send_x, 'expert', split_axis=0, concat_axis=0, tiled=True)]
    all_to_all x1 -> x0, waiting for transfers between devices: 14.8 us -> none  [local(): lax.all_to_all(whole.reshape(experts, capacity, width), 'expert', split_a...]
    dot_general x6 -> x0, matrix products: 9.94 us -> none  [the longest x1 2.64 us: local(): lax.dot_general(x_rows, gate_part, contract, preferred_element_type=jnp.f...]
    all_to_all x1 -> x0, starting transfers between devices: 4.78 us -> none  [local(): lax.all_to_all(whole.reshape(experts, capacity, width), 'expert', split_a...]
    unnamed x21 -> x13, local copies, waits for them, and re-layouts: 1.99 us -> 5.73 us
    gather x3 -> x0, local copies, waits for them, and re-layouts: 3.58 us -> none  [the longest x1 2.03 us: local(): send_x = jnp.take(x_pad, source, axis=0).reshape(experts, capacity, width)]
  transfers between devices with their start and end apart: 3 -> 0, of which waited for: 3 -> 0; matrix products, arithmetic and copies ran while one was open for 2% -> 0% of each run, Pallas kernels for 0% -> 0%
where the time goes in v1:
time: 92.3 us; the launch traced here: 92 us
  Pallas kernels  84.5 us (92%)
  local copies, waits for them, and re-layouts  6.07 us (7%)
    pallas_call x1, Pallas kernels, local(): pl.pallas_call(lambda *refs: kernel((ns, ne, nd), *refs), out_shape=(jax....  84.5 us
    unnamed x13, local copies, waits for them, and re-layouts  5.73 us

profile of v1, /device:TPU:24, one launch (start us, length us, event | category | flops | bytes accessed | tf_op | source)
XLA Modules:
  0.0 92.0 jit_solution(9840788040966019681)
XLA Ops:
  0.6 0.0 copy-start.3
  0.6 0.7 copy-done.3
  1.3 0.1 copy.11
  1.4 0.1 eq.15
  1.6 0.2 convert_reduce_fusion
  1.7 0.1 reduce_sum.12
  1.9 0.1 copy.12
  2.0 0.6 add_bitcast_fusion.refs_1_
  2.6 84.5 %shard_map.84 = (bf16[512,512]{1,0:T(8,128)(2,1)}, bf16[16,8,768]{2,1,0:T(8,128)(2,1)}, bf16[768,512]{1,0:T(8,128)(2,1)}, bf16[768,512]{1,0:T(8,128)(2,1)}) custom-call(bf16[128,768]{1,0:T(8,128)(2,1)} %refs_0_.1, s32[2,128]{1,0:T(2,128)} %add_bitcast_fusion.refs_1_, bf16[768,512]{1,0:T(8,128)(2,1)} %bitcast.11, bf16[768,512]{1,0:T(8,128)(2,1)} %bitcast.12, ...), custom_call_target="tpu_custom_call" | custom-call | tf_op jit(solution)/shard_map/pallas_call | solution.py:241
  87.1 0.0 copy-start.1
  87.1 0.0 copy-start.2
  87.1 2.0 %copy.17 = bf16[1,512,512]{2,1,0:T(8,128)(2,1)} copy(bf16[1,512,512]{2,1,0:T(8,128)(2,1)} %bitcast.13) | data formatting | bytes 1048576
  89.1 0.0 copy-done.2
  89.1 0.7 copy.18
  89.7 0.0 copy-done.1
  89.7 0.0 copy-start
  89.7 0.9 copy.19
  90.6 0.5 copy-done
  91.2 0.9 copy.20
Async XLA Ops:
  0.6 0.7 copy-start.3
  87.1 2.7 %copy-start.1 = (bf16[768,512]{1,0:T(8,128)(2,1)S(1)}, bf16[768,512]{1,0:T(8,128)(2,1)}, u32[]{:S(2)}) copy-start(bf16[768,512]{1,0:T(8,128)(2,1)} %get-tuple-element.10) | copy-start | bytes 2359300
  87.1 2.0 %copy-start.2 = (bf16[16,8,768]{2,1,0:T(8,128)(2,1)S(1)}, bf16[16,8,768]{2,1,0:T(8,128)(2,1)}, u32[]{:S(2)}) copy-start(bf16[16,8,768]{2,1,0:T(8,128)(2,1)} %get-tuple-element.9) | copy-start | bytes 589828
  89.7 1.4 %copy-start = (bf16[768,512]{1,0:T(8,128)(2,1)S(1)}, bf16[768,512]{1,0:T(8,128)(2,1)}, u32[]{:S(2)}) copy-start(bf16[768,512]{1,0:T(8,128)(2,1)} %get-tuple-element.11) | copy-start | bytes 2359300

commit v2 on v1

--- a/solution.py
+++ b/solution.py
@@ -18,11 +18,13 @@
 
 def kernel(
     sizes,
-    tok, slots, wg, wu, cot,
-    acted, grad_in, grad_gate, grad_up,
-    pick, x_out, x_all, pre_out, pre_in, pre_own, pre_all,
-    gate_part, up_part, back_out, home, whole, z_out, z_in, z_all,
-    x_ss, x_rs, p_ss, p_rs, a_ss, a_rs, h_ss, h_rs, zr_ss, zr_rs, za_ss, za_rs,
+    tok, ids, wg_hbm, wu_hbm, cot_hbm,
+    acted_hbm, grad_in, gate_hbm, up_hbm,
+    wg, wu, cot, acted, grad_gate, grad_up,
+    pick, x_out, x_all, pre_out, pre_in, pre_own, parts,
+    back_out, home, whole, z_out, z_in, z_all,
+    in_sem, out_sem,
+    x_ss, x_rs, p_ss, p_rs, a_ss, a_rs, o_ss, o_rs, h_ss, h_rs, zr_ss, zr_rs, za_ss, za_rs,
 ):
     ns, ne, nd = sizes
     s, e, d = lax.axis_index("section"), lax.axis_index("expert"), lax.axis_index("dp")
@@ -52,10 +54,28 @@
                 device_id_type=pl.DeviceIdType.MESH,
             )
 
-    at = lax.broadcasted_iota(jnp.int32, pick.shape, 0)
-    pick[...] = jnp.where(
-        (at == slots[0:1, :]) | (at == slots[1:2, :]), 1.0, 0.0
-    ).astype(BF16)
+    loads = [
+        pltpu.make_async_copy(src, dst, in_sem.at[i])
+        for i, (src, dst) in enumerate(((wg_hbm, wg), (wu_hbm, wu), (cot_hbm, cot)))
+    ]
+    for copy in loads:
+        copy.start()
+
+    count = tok.shape[0]
+    named = lax.broadcasted_iota(jnp.int32, (ne, count), 0)
+    member = (named == ids[0:1, :]) | (named == ids[1:2, :])
+    before = lax.broadcasted_iota(jnp.int32, (count, count), 0) < lax.broadcasted_iota(
+        jnp.int32, (count, count), 1
+    )
+    rank = dot(
+        jnp.where(member, 1.0, 0.0).astype(BF16), jnp.where(before, 1.0, 0.0).astype(BF16), NN
+    ).astype(jnp.int32)
+    rank = jnp.where(member, rank, -1)
+    at = lax.broadcasted_iota(jnp.int32, (cap, count), 0)
+    for g in range(ne):
+        pick[g * cap : (g + 1) * cap, :] = jnp.where(at == rank[g : g + 1, :], 1.0, 0.0).astype(
+            BF16
+        )
 
     def build(g, _):
         x_out[rows(g), :] = dot(pick[rows(g), :], tok[...], NN).astype(BF16)
@@ -80,10 +100,14 @@
             pre_out.at[rows(g)], pre_in.at[i, d], p_ss.at[g], p_rs.at[i, d], "dp", g % nd
         )
 
-    def forward(k, _):
+    for copy in loads[:2]:
+        copy.wait()
+
+    def forward(t, _):
+        k = jnp.where(t < 4, t, jnp.where(t < 6, t + 2, t - 2))
         g = expert_peer(k)
 
-        @pl.when(k > 0)
+        @pl.when(t > 0)
         def _():
             x_copy(g, g).wait_recv()
 
@@ -106,12 +130,21 @@
 
     lax.fori_loop(0, ne, forward, 0)
 
-    def a_copy(i, peer, g):
-        return send(
-            pre_all.at[rows(g)], pre_all.at[rows(g)], a_ss.at[i, peer], a_rs.at[g], "dp", peer
-        )
-
-    def owned(i, _):
+    def a_copy(peer, g):
+        return send(
+            parts.at[rows(g)], parts.at[rows(g)], a_ss.at[g // nd, peer], a_rs.at[g], "dp", peer
+        )
+
+    def o_copy(peer, g):
+        return send(
+            acted.at[rows(g)], acted.at[rows(g)], o_ss.at[g // nd, peer], o_rs.at[g], "dp", peer
+        )
+
+    loads[2].wait()
+    first = y // (ny // per)
+
+    def owned(t, _):
+        i = (first + t) % per
         total = pre_own[i]
         for k in range(1, nd):
             src = (d + k) % nd
@@ -120,44 +153,44 @@
             ).wait_recv()
             total = total + pre_in[i, src].astype(F32)
         g = i * nd + d
-        pre_all[rows(g), :] = total.astype(BF16)
-        for k in range(1, nd):
-            a_copy(i, (d + k) % nd, g).start()
-        return 0
-
-    lax.fori_loop(0, per, owned, 0)
-
-    def h_copy(g):
-        return send(back_out.at[rows(g)], home.at[rows(e)], h_ss.at[g], h_rs.at[e], "expert", g)
-
-    def backward(t, _):
-        i, k = t // nd, t % nd
-        src = (d + k) % nd
-        g = i * nd + src
-
-        @pl.when(k > 0)
-        def _():
-            a_copy(i, src, g).wait_recv()
-
-        pre_gate = pre_all[rows(g), :hid].astype(F32)
-        pre_up = pre_all[rows(g), hid:].astype(F32)
+        pre_gate, pre_up = total[:, :hid], total[:, hid:]
         cf = cot[rows(g), :].astype(F32)
         sig = jax.nn.sigmoid(pre_gate)
         silu = pre_gate * sig
+        gp = cf * pre_up * sig * (1.0 + pre_gate * (1.0 - sig))
+        parts[rows(g), :hid] = gp.astype(BF16)
+        parts[rows(g), hid:] = (cf * silu).astype(BF16)
         acted[rows(g), :] = (silu * pre_up).astype(BF16)
-        gp = (cf * pre_up * sig * (1.0 + pre_gate * (1.0 - sig))).astype(BF16)
-        up = (cf * silu).astype(BF16)
-        gate_part[rows(g), :] = gp
-        up_part[rows(g), :] = up
-        back = (dot(gp, wg[...], NT) + dot(up, wu[...], NT)).astype(BF16)
+        for k in range(1, nd):
+            a_copy((d + k) % nd, g).start()
+        return 0
+
+    lax.fori_loop(0, per, owned, 0)
+    for i in range(per):
+        for k in range(1, nd):
+            o_copy((d + k) % nd, i * nd + d).start()
+
+    def h_copy(g):
+        return send(back_out.at[rows(g)], home.at[rows(e)], h_ss.at[g], h_rs.at[e], "expert", g)
+
+    def backward(t, _):
+        k = t % nd
+        src = (d + k) % nd
+        g = (first + t // nd) % per * nd + src
+
+        @pl.when(k > 0)
+        def _():
+            a_copy(src, g).wait_recv()
+
+        back = dot(parts[rows(g), :hid], wg[...], NT) + dot(parts[rows(g), hid:], wu[...], NT)
 
         @pl.when(g == e)
         def _():
-            home[rows(g), :] = back
+            home[rows(g), :] = back.astype(BF16)
 
         @pl.when(g != e)
         def _():
-            back_out[rows(g), :] = back
+            back_out[rows(g), :] = back.astype(BF16)
             h_copy(g).start()
 
         return 0
@@ -169,11 +202,19 @@
     def weights(i, _):
         at = pl.ds(pl.multiple_of(i * tile, tile), tile)
         x = x_all[:, at]
-        grad_gate[at, :] = dot(x, gate_part[...], TN).astype(BF16)
-        grad_up[at, :] = dot(x, up_part[...], TN).astype(BF16)
+        grad_gate[at, :] = dot(x, parts[:, :hid], TN).astype(BF16)
+        grad_up[at, :] = dot(x, parts[:, hid:], TN).astype(BF16)
         return 0
 
     lax.fori_loop(0, wg.shape[0] // tile, weights, 0)
+    stores = [
+        pltpu.make_async_copy(src, dst, out_sem.at[i])
+        for i, (src, dst) in enumerate(
+            ((grad_gate, gate_hbm), (grad_up, up_hbm), (acted, acted_hbm))
+        )
+    ]
+    for copy in stores[:2]:
+        copy.start()
 
     for k in range(1, ne):
         src = expert_peer(k)
@@ -206,6 +247,11 @@
     z_all[s] = total.astype(BF16)
     for k in far:
         za_copy((s + k) % ns, s).start()
+    for i in range(per):
+        for k in range(1, nd):
+            src = (d + k) % nd
+            o_copy(src, i * nd + src).wait_recv()
+    stores[2].start()
     for k in reversed(far):
         src = (s + k) % ns
         za_copy(src, src).wait_recv()
@@ -217,10 +263,27 @@
     for i in range(per):
         for k in range(1, nd):
             p_copy(i * nd + (d + k) % nd).wait_send()
-            a_copy(i, (d + k) % nd, i * nd + d).wait_send()
+            a_copy((d + k) % nd, i * nd + d).wait_send()
+            o_copy((d + k) % nd, i * nd + d).wait_send()
     for k in far:
         zr_copy((s + k) % ns, s).wait_send()
         za_copy((s + k) % ns, s).wait_send()
+    for copy in stores:
+        copy.wait()
+
+
+def settle(*refs):
+    n = (len(refs) - 2) // 3
+    src, dst, held, (in_sem, out_sem) = refs[:n], refs[n : 2 * n], refs[2 * n : 3 * n], refs[3 * n :]
+    reads = [pltpu.make_async_copy(src[i], held[i], in_sem.at[i]) for i in range(n)]
+    writes = [pltpu.make_async_copy(held[i], dst[i], out_sem.at[i]) for i in range(n)]
+    for copy in reads:
+        copy.start()
+    for i in range(n):
+        reads[i].wait()
+        writes[i].start()
+    for copy in writes:
+        copy.wait()
 
 
 def local(tokens, expert_ids, w_gate, w_up, cotangent):
@@ -229,16 +292,11 @@
     hid = w_gate.shape[2]
     slots = cotangent.shape[1]
     cap = slots // ne
-    flat = expert_ids.reshape(-1)
-    order = jnp.arange(2 * count, dtype=jnp.int32)
-    earlier = (flat[:, None] == flat[None, :]) & (order[None, :] < order[:, None])
-    slot = flat * cap + jnp.sum(earlier.astype(jnp.int32), axis=1)
-    slot = slot.reshape(count, 2).T
-
     vmem = pl.BlockSpec(memory_space=pltpu.VMEM)
     dma = pltpu.SemaphoreType.DMA
     share = count // ns
-    acted, grad_in, grad_gate, grad_up = pl.pallas_call(
+    anywhere = pl.BlockSpec(memory_space=pl.ANY)
+    outs = pl.pallas_call(
         lambda *refs: kernel((ns, ne, nd), *refs),
         out_shape=(
             jax.ShapeDtypeStruct((slots, hid), BF16),
@@ -246,9 +304,15 @@
             jax.ShapeDtypeStruct((width, hid), BF16),
             jax.ShapeDtypeStruct((width, hid), BF16),
         ),
-        in_specs=[vmem] * 5,
-        out_specs=(vmem,) * 4,
+        in_specs=[vmem] * 2 + [anywhere] * 3,
+        out_specs=(anywhere, vmem, anywhere, anywhere),
         scratch_shapes=[
+            pltpu.VMEM((width, hid), BF16),
+            pltpu.VMEM((width, hid), BF16),
+            pltpu.VMEM((slots, hid), BF16),
+            pltpu.VMEM((slots, hid), BF16),
+            pltpu.VMEM((width, hid), BF16),
+            pltpu.VMEM((width, hid), BF16),
             pltpu.VMEM((slots, count), BF16),
             pltpu.VMEM((slots, width), BF16),
             pltpu.VMEM((slots, width), BF16),
@@ -256,23 +320,31 @@
             pltpu.VMEM((ne // nd, nd, cap, 2 * hid), BF16),
             pltpu.VMEM((ne // nd, cap, 2 * hid), F32),
             pltpu.VMEM((slots, 2 * hid), BF16),
-            pltpu.VMEM((slots, hid), BF16),
-            pltpu.VMEM((slots, hid), BF16),
             pltpu.VMEM((slots, width), BF16),
             pltpu.VMEM((slots, width), BF16),
             pltpu.VMEM((ns, share, width), F32),
             pltpu.VMEM((ns, share, width), BF16),
             pltpu.VMEM((ns, share, width), BF16),
             pltpu.VMEM((ns, share, width), BF16),
+            dma((3,)), dma((3,)),
             dma((ne,)), dma((ne,)),
             dma((ne,)), dma((ne // nd, nd)),
+            dma((ne // nd, nd)), dma((ne,)),
             dma((ne // nd, nd)), dma((ne,)),
             dma((ne,)), dma((ne,)),
             dma((ns,)), dma((ns,)),
             dma((ns,)), dma((ns,)),
         ],
         compiler_params=pltpu.CompilerParams(collective_id=0, has_side_effects=True),
-    )(tokens, slot, w_gate[0], w_up[0], cotangent[0])
+    )(tokens, expert_ids.T, w_gate[0], w_up[0], cotangent[0])
+    n = len(outs)
+    acted, grad_in, grad_gate, grad_up = pl.pallas_call(
+        settle,
+        out_shape=tuple(jax.ShapeDtypeStruct(o.shape, o.dtype) for o in outs),
+        in_specs=[anywhere] * n,
+        out_specs=(anywhere,) * n,
+        scratch_shapes=[pltpu.VMEM(o.shape, o.dtype) for o in outs] + [dma((n,)), dma((n,))],
+    )(*outs)
     return acted[None], grad_in.reshape(count, width), grad_gate[None], grad_up[None]
 
 

time: 92.3 us -> 88.4 us (0.958); the launches traced: 92 us -> 86.9 us
  local copies, waits for them, and re-layouts: 6.07 us -> 0 us
  Pallas kernels: 84.5 us -> 86.3 us
    unnamed x13 -> x0, local copies, waits for them, and re-layouts: 5.73 us -> none
    pallas_call x0 -> x1, Pallas kernels: none -> 2.56 us  [local(): pl.pallas_call(settle, out_shape=tuple((jax.ShapeDtypeStruct(o.shape, o.d...]
where the time goes in v2:
time: 88.4 us; the launch traced here: 86.9 us
  Pallas kernels  86.3 us (98%)
    pallas_call x1, Pallas kernels, local(): pl.pallas_call(lambda *refs: kernel((ns, ne, nd), *refs), out_shape=(jax....  83.7 us
    pallas_call x1, Pallas kernels, local(): pl.pallas_call(settle, out_shape=tuple((jax.ShapeDtypeStruct(o.shape, o.d...  2.56 us

profile of v2, /device:TPU:24, one launch (start us, length us, event | category | flops | bytes accessed | tf_op | source)
XLA Modules:
  0.0 86.9 jit_solution(3740012277381219685)
XLA Ops:
  0.6 83.7 %shard_map.84 = (bf16[512,512]{1,0:T(8,128)(2,1)}, bf16[16,8,768]{2,1,0:T(8,128)(2,1)}, bf16[768,512]{1,0:T(8,128)(2,1)}, bf16[768,512]{1,0:T(8,128)(2,1)}) custom-call(bf16[128,768]{1,0:T(8,128)(2,1)} %refs_0_.1, s32[2,128]{1,0:T(2,128)} %bitcast.11, bf16[768,512]{1,0:T(8,128)(2,1)} %bitcast.8, bf16[768,512]{1,0:T(8,128)(2,1)} %bitcast.9, ...), custom_call_target="tpu_custom_call" | custom-call | tf_op jit(solution)/shard_map/pallas_call | solution.py:299
  84.4 2.6 %shard_map.85 = (bf16[512,512]{1,0:T(8,128)(2,1)}, bf16[16,8,768]{2,1,0:T(8,128)(2,1)}, bf16[768,512]{1,0:T(8,128)(2,1)}, bf16[768,512]{1,0:T(8,128)(2,1)}) custom-call(bf16[512,512]{1,0:T(8,128)(2,1)} %get-tuple-element.12.refs_0_, bf16[16,8,768]{2,1,0:T(8,128)(2,1)} %get-tuple-element.13.refs_1_, bf16[768,512]{1,0:T(8,128)(2,1)} %get-tuple-element.14.refs_2_, ...), custom_call_target="tpu_custom_call" | custom-call | tf_op jit(solution)/shard_map/pallas_call | solution.py:341

commit v3 on v2

--- a/solution.py
+++ b/solution.py
@@ -24,7 +24,7 @@
     pick, x_out, x_all, pre_out, pre_in, pre_own, parts,
     back_out, home, whole, z_out, z_in, z_all,
     in_sem, out_sem,
-    x_ss, x_rs, p_ss, p_rs, a_ss, a_rs, o_ss, o_rs, h_ss, h_rs, zr_ss, zr_rs, za_ss, za_rs,
+    x_ss, x_rs, p_ss, p_rs, a_ss, a_rs, f_ss, f_rs, o_ss, o_rs, h_ss, h_rs, zr_ss, zr_rs, za_ss, za_rs,
 ):
     ns, ne, nd = sizes
     s, e, d = lax.axis_index("section"), lax.axis_index("expert"), lax.axis_index("dp")
@@ -91,7 +91,8 @@
             "expert", peer,
         )
 
-    for k in range(1, ne):
+    near, two_away = (1, 2, 3, 6, 7), (4, 5)
+    for k in near:
         x_copy(expert_peer(k), e).start()
 
     def p_copy(g):
@@ -128,11 +129,26 @@
 
         return 0
 
-    lax.fori_loop(0, ne, forward, 0)
-
-    def a_copy(peer, g):
-        return send(
-            parts.at[rows(g)], parts.at[rows(g)], a_ss.at[g // nd, peer], a_rs.at[g], "dp", peer
+    lax.fori_loop(0, 2, forward, 0)
+    for k in near:
+        x_copy(expert_peer(k), e).wait_send()
+    for k in two_away:
+        x_copy(expert_peer(k), e).start()
+    lax.fori_loop(2, ne, forward, 0)
+
+    right, left = (d + 1) % nd, (d + nd - 1) % nd
+
+    def a_copy(side, g):
+        return send(
+            parts.at[rows(g)], parts.at[rows(g)], a_ss.at[g // nd, side], a_rs.at[g],
+            "dp", left if side else right,
+        )
+
+    def f_copy(side, g):
+        part = pl.ds(pl.multiple_of(g * cap + side * (cap // 2), cap // 2), cap // 2)
+        return send(
+            parts.at[part], parts.at[part], f_ss.at[g // nd, side], f_rs.at[g, side],
+            "dp", left if side else right,
         )
 
     def o_copy(peer, g):
@@ -143,8 +159,7 @@
     loads[2].wait()
     first = y // (ny // per)
 
-    def owned(t, _):
-        i = (first + t) % per
+    def owned(i):
         total = pre_own[i]
         for k in range(1, nd):
             src = (d + k) % nd
@@ -161,41 +176,51 @@
         parts[rows(g), :hid] = gp.astype(BF16)
         parts[rows(g), hid:] = (cf * silu).astype(BF16)
         acted[rows(g), :] = (silu * pre_up).astype(BF16)
-        for k in range(1, nd):
-            a_copy((d + k) % nd, g).start()
+        for side in range(2):
+            a_copy(side, g).start()
+
+    def h_copy(g):
+        return send(back_out.at[rows(g)], home.at[rows(e)], h_ss.at[g], h_rs.at[e], "expert", g)
+
+    def backward(i, k):
+        g = i * nd + (d + k) % nd
+        if k == 1:
+            a_copy(0, g).wait_recv()
+            f_copy(1, g).start()
+        elif k == nd - 1:
+            a_copy(0, g).wait_recv()
+            f_copy(0, g).start()
+        elif k > 0:
+            f_copy(0, g).wait_recv()
+            f_copy(1, g).wait_recv()
+        back = dot(parts[rows(g), :hid], wg[...], NT) + dot(parts[rows(g), hid:], wu[...], NT)
+
+        @pl.when(g == e)
+        def _():
+            home[rows(g), :] = back.astype(BF16)
+
+        @pl.when(g != e)
+        def _():
+            back_out[rows(g), :] = back.astype(BF16)
+            h_copy(g).start()
+
+    def wave(t, _):
+        i = (first + t) % per
+        owned(i)
+
+        @pl.when(t > 0)
+        def _():
+            backward((first + t + per - 1) % per, 2)
+
+        for k in (0, 1, 3):
+            backward(i, k)
         return 0
 
-    lax.fori_loop(0, per, owned, 0)
+    lax.fori_loop(0, per, wave, 0)
+    backward((first + per - 1) % per, 2)
     for i in range(per):
         for k in range(1, nd):
             o_copy((d + k) % nd, i * nd + d).start()
-
-    def h_copy(g):
-        return send(back_out.at[rows(g)], home.at[rows(e)], h_ss.at[g], h_rs.at[e], "expert", g)
-
-    def backward(t, _):
-        k = t % nd
-        src = (d + k) % nd
-        g = (first + t // nd) % per * nd + src
-
-        @pl.when(k > 0)
-        def _():
-            a_copy(src, g).wait_recv()
-
-        back = dot(parts[rows(g), :hid], wg[...], NT) + dot(parts[rows(g), hid:], wu[...], NT)
-
-        @pl.when(g == e)
-        def _():
-            home[rows(g), :] = back.astype(BF16)
-
-        @pl.when(g != e)
-        def _():
-            back_out[rows(g), :] = back.astype(BF16)
-            h_copy(g).start()
-
-        return 0
-
-    lax.fori_loop(0, ne, backward, 0)
 
     tile = 128
 
@@ -257,14 +282,17 @@
         za_copy(src, src).wait_recv()
     grad_in[...] = z_all[...]
 
+    for k in two_away:
+        x_copy(expert_peer(k), e).wait_send()
     for k in range(1, ne):
-        x_copy(expert_peer(k), e).wait_send()
         h_copy(expert_peer(k)).wait_send()
     for i in range(per):
         for k in range(1, nd):
             p_copy(i * nd + (d + k) % nd).wait_send()
-            a_copy((d + k) % nd, i * nd + d).wait_send()
             o_copy((d + k) % nd, i * nd + d).wait_send()
+        for side in range(2):
+            a_copy(side, i * nd + d).wait_send()
+            f_copy(side, i * nd + d).wait_send()
     for k in far:
         zr_copy((s + k) % ns, s).wait_send()
         za_copy((s + k) % ns, s).wait_send()
@@ -275,13 +303,23 @@
 def settle(*refs):
     n = (len(refs) - 2) // 3
     src, dst, held, (in_sem, out_sem) = refs[:n], refs[n : 2 * n], refs[2 * n : 3 * n], refs[3 * n :]
-    reads = [pltpu.make_async_copy(src[i], held[i], in_sem.at[i]) for i in range(n)]
-    writes = [pltpu.make_async_copy(held[i], dst[i], out_sem.at[i]) for i in range(n)]
+    pieces = in_sem.shape[1]
+    reads, writes = [], []
+    for i in range(n):
+        size = src[i].shape[0] // pieces
+        for p in range(pieces):
+            at = pl.ds(p * size, size)
+            reads.append(
+                pltpu.make_async_copy(src[i].at[at], held[i].at[at], in_sem.at[i, p])
+            )
+            writes.append(
+                pltpu.make_async_copy(held[i].at[at], dst[i].at[at], out_sem.at[i, p])
+            )
     for copy in reads:
         copy.start()
-    for i in range(n):
-        reads[i].wait()
-        writes[i].start()
+    for read, write in zip(reads, writes):
+        read.wait()
+        write.start()
     for copy in writes:
         copy.wait()
 
@@ -329,7 +367,8 @@
             dma((3,)), dma((3,)),
             dma((ne,)), dma((ne,)),
             dma((ne,)), dma((ne // nd, nd)),
-            dma((ne // nd, nd)), dma((ne,)),
+            dma((ne // nd, 2)), dma((ne,)),
+            dma((ne // nd, 2)), dma((ne, 2)),
             dma((ne // nd, nd)), dma((ne,)),
             dma((ne,)), dma((ne,)),
             dma((ns,)), dma((ns,)),
@@ -343,7 +382,7 @@
         out_shape=tuple(jax.ShapeDtypeStruct(o.shape, o.dtype) for o in outs),
         in_specs=[anywhere] * n,
         out_specs=(anywhere,) * n,
-        scratch_shapes=[pltpu.VMEM(o.shape, o.dtype) for o in outs] + [dma((n,)), dma((n,))],
+        scratch_shapes=[pltpu.VMEM(o.shape, o.dtype) for o in outs] + [dma((n, 4)), dma((n, 4))],
     )(*outs)
     return acted[None], grad_in.reshape(count, width), grad_gate[None], grad_up[None]
 

time: 88.4 us -> 84 us (0.950)
  the two profiles are of different devices: /device:TPU:24 before, /device:TPU:11 now
where the time goes in v3:
time: 84 us; the launch traced here: 83.8 us
  Pallas kernels  83.2 us (99%)
    pallas_call x1, Pallas kernels, local(): pl.pallas_call(lambda *refs: kernel((ns, ne, nd), *refs), out_shape=(jax....  80.5 us
    pallas_call x1, Pallas kernels, local(): pl.pallas_call(settle, out_shape=tuple((jax.ShapeDtypeStruct(o.shape, o.d...  2.66 us

profile of v3, /device:TPU:11, one launch (start us, length us, event | category | flops | bytes accessed | tf_op | source)
XLA Modules:
  0.0 83.8 jit_solution(13845678478282154073)
XLA Ops:
  0.6 80.5 %shard_map.84 = (bf16[512,512]{1,0:T(8,128)(2,1)}, bf16[16,8,768]{2,1,0:T(8,128)(2,1)}, bf16[768,512]{1,0:T(8,128)(2,1)}, bf16[768,512]{1,0:T(8,128)(2,1)}) custom-call(bf16[128,768]{1,0:T(8,128)(2,1)} %refs_0_.1, s32[2,128]{1,0:T(2,128)} %bitcast.11, bf16[768,512]{1,0:T(8,128)(2,1)} %bitcast.8, bf16[768,512]{1,0:T(8,128)(2,1)} %bitcast.9, ...), custom_call_target="tpu_custom_call" | custom-call | tf_op jit(solution)/shard_map/pallas_call | solution.py:337
  81.1 2.7 %shard_map.85 = (bf16[512,512]{1,0:T(8,128)(2,1)}, bf16[16,8,768]{2,1,0:T(8,128)(2,1)}, bf16[768,512]{1,0:T(8,128)(2,1)}, bf16[768,512]{1,0:T(8,128)(2,1)}) custom-call(bf16[512,512]{1,0:T(8,128)(2,1)} %get-tuple-element.12.refs_0_, bf16[16,8,768]{2,1,0:T(8,128)(2,1)} %get-tuple-element.13.refs_1_, bf16[768,512]{1,0:T(8,128)(2,1)} %get-tuple-element.14.refs_2_, ...), custom_call_target="tpu_custom_call" | custom-call | tf_op jit(solution)/shard_map/pallas_call | solution.py:380

commit v4 on v3

--- a/solution.py
+++ b/solution.py
@@ -23,7 +23,7 @@
     wg, wu, cot, acted, grad_gate, grad_up,
     pick, x_out, x_all, pre_out, pre_in, pre_own, parts,
     back_out, home, whole, z_out, z_in, z_all,
-    in_sem, out_sem,
+    in_sem, out_sem, known,
     x_ss, x_rs, p_ss, p_rs, a_ss, a_rs, f_ss, f_rs, o_ss, o_rs, h_ss, h_rs, zr_ss, zr_rs, za_ss, za_rs,
 ):
     ns, ne, nd = sizes
@@ -47,8 +47,10 @@
         )
 
     barrier = pltpu.get_barrier_semaphore()
-    for axis, me, n in (("section", s, ns), ("expert", e, ne), ("dp", d, nd)):
-        for k in range(1, n):
+    rounds = ns // 2 - 1
+    greeted = (("section", s, ns, (1, ns - 1)), ("expert", e, ne, range(1, ne)), ("dp", d, nd, range(1, nd)))
+    for axis, me, n, offsets in greeted:
+        for k in offsets:
             pl.semaphore_signal(
                 barrier, inc=1, device_id={axis: (me + k) % n},
                 device_id_type=pl.DeviceIdType.MESH,
@@ -77,13 +79,8 @@
             BF16
         )
 
-    def build(g, _):
+    def build(g):
         x_out[rows(g), :] = dot(pick[rows(g), :], tok[...], NN).astype(BF16)
-        return 0
-
-    lax.fori_loop(0, ne, build, 0)
-    x_all[rows(e), :] = x_out[rows(e), :]
-    pl.semaphore_wait(barrier, ns + ne + nd - 3)
 
     def x_copy(peer, slot):
         return send(
@@ -91,9 +88,29 @@
             "expert", peer,
         )
 
-    near, two_away = (1, 2, 3, 6, 7), (4, 5)
-    for k in near:
+    near, two_away = (2, 3, 6, 7, 1), (4, 5)
+    build(expert_peer(near[0]))
+    pl.semaphore_wait(barrier, sum(len(g[3]) for g in greeted))
+    for n, k in enumerate(near):
+        if n:
+            build(expert_peer(k))
         x_copy(expert_peer(k), e).start()
+    x_all[rows(e), :] = dot(pick[rows(e), :], tok[...], NN).astype(BF16)
+    for k in two_away:
+        build(expert_peer(k))
+
+    def spread(t):
+        @pl.when((t > 0) & (t <= rounds))
+        def _():
+            pl.semaphore_wait(known.at[t - 1], 2)
+
+        @pl.when(t < rounds)
+        def _():
+            for k in (1, ns - 1):
+                pl.semaphore_signal(
+                    known.at[t], inc=1, device_id={"section": (s + k) % ns},
+                    device_id_type=pl.DeviceIdType.MESH,
+                )
 
     def p_copy(g):
         i = g // nd
@@ -105,6 +122,7 @@
         copy.wait()
 
     def forward(t, _):
+        spread(t)
         k = jnp.where(t < 4, t, jnp.where(t < 6, t + 2, t - 2))
         g = expert_peer(k)
 
@@ -364,7 +382,7 @@
             pltpu.VMEM((ns, share, width), BF16),
             pltpu.VMEM((ns, share, width), BF16),
             pltpu.VMEM((ns, share, width), BF16),
-            dma((3,)), dma((3,)),
+            dma((3,)), dma((3,)), pltpu.SemaphoreType.REGULAR((ns // 2 - 1,)),
             dma((ne,)), dma((ne,)),
             dma((ne,)), dma((ne // nd, nd)),
             dma((ne // nd, 2)), dma((ne,)),

time: 84 us -> 82.1 us (0.977)
  the two profiles are of different devices: /device:TPU:11 before, /device:TPU:10 now
where the time goes in v4:
time: 82.1 us; the launch traced here: 81.9 us
  Pallas kernels  81.3 us (99%)
    pallas_call x1, Pallas kernels, local(): pl.pallas_call(lambda *refs: kernel((ns, ne, nd), *refs), out_shape=(jax....  78.6 us
    pallas_call x1, Pallas kernels, local(): pl.pallas_call(settle, out_shape=tuple((jax.ShapeDtypeStruct(o.shape, o.d...  2.66 us

profile of v4, /device:TPU:10, one launch (start us, length us, event | category | flops | bytes accessed | tf_op | source)
XLA Modules:
  0.0 81.9 jit_solution(8165745560427654770)
XLA Ops:
  0.6 78.6 %shard_map.84 = (bf16[512,512]{1,0:T(8,128)(2,1)}, bf16[16,8,768]{2,1,0:T(8,128)(2,1)}, bf16[768,512]{1,0:T(8,128)(2,1)}, bf16[768,512]{1,0:T(8,128)(2,1)}) custom-call(bf16[128,768]{1,0:T(8,128)(2,1)} %refs_0_.1, s32[2,128]{1,0:T(2,128)} %bitcast.11, bf16[768,512]{1,0:T(8,128)(2,1)} %bitcast.8, bf16[768,512]{1,0:T(8,128)(2,1)} %bitcast.9, ...), custom_call_target="tpu_custom_call" | custom-call | tf_op jit(solution)/shard_map/pallas_call | solution.py:355
  79.2 2.7 %shard_map.85 = (bf16[512,512]{1,0:T(8,128)(2,1)}, bf16[16,8,768]{2,1,0:T(8,128)(2,1)}, bf16[768,512]{1,0:T(8,128)(2,1)}, bf16[768,512]{1,0:T(8,128)(2,1)}) custom-call(bf16[512,512]{1,0:T(8,128)(2,1)} %get-tuple-element.12.refs_0_, bf16[16,8,768]{2,1,0:T(8,128)(2,1)} %get-tuple-element.13.refs_1_, bf16[768,512]{1,0:T(8,128)(2,1)} %get-tuple-element.14.refs_2_, ...), custom_call_target="tpu_custom_call" | custom-call | tf_op jit(solution)/shard_map/pallas_call | solution.py:398

commit v5 on v4

--- a/solution.py
+++ b/solution.py
@@ -123,7 +123,9 @@
 
     def forward(t, _):
         spread(t)
-        k = jnp.where(t < 4, t, jnp.where(t < 6, t + 2, t - 2))
+        k = jnp.where(
+            t < 2, t, jnp.where(t < 4, 4 * (y % 2) + t, jnp.where(t < 6, 2 - 4 * (y % 2) + t, t - 2))
+        )
         g = expert_peer(k)
 
         @pl.when(t > 0)
@@ -143,9 +145,19 @@
         def _():
             pre_out[rows(g), :hid] = pg.astype(BF16)
             pre_out[rows(g), hid:] = pu.astype(BF16)
+
+        @pl.when(t == ne // 2)
+        def _():
+            for k in range(1, nd):
+                p_copy(first * nd + (d + k) % nd).wait_send()
+
+        @pl.when(g % nd != d)
+        def _():
             p_copy(g).start()
 
         return 0
+
+    first = y // (ny // per)
 
     lax.fori_loop(0, 2, forward, 0)
     for k in near:
@@ -175,7 +187,6 @@
         )
 
     loads[2].wait()
-    first = y // (ny // per)
 
     def owned(i):
         total = pre_own[i]
@@ -240,25 +251,6 @@
         for k in range(1, nd):
             o_copy((d + k) % nd, i * nd + d).start()
 
-    tile = 128
-
-    def weights(i, _):
-        at = pl.ds(pl.multiple_of(i * tile, tile), tile)
-        x = x_all[:, at]
-        grad_gate[at, :] = dot(x, parts[:, :hid], TN).astype(BF16)
-        grad_up[at, :] = dot(x, parts[:, hid:], TN).astype(BF16)
-        return 0
-
-    lax.fori_loop(0, wg.shape[0] // tile, weights, 0)
-    stores = [
-        pltpu.make_async_copy(src, dst, out_sem.at[i])
-        for i, (src, dst) in enumerate(
-            ((grad_gate, gate_hbm), (grad_up, up_hbm), (acted, acted_hbm))
-        )
-    ]
-    for copy in stores[:2]:
-        copy.start()
-
     for k in range(1, ne):
         src = expert_peer(k)
         send(
@@ -282,6 +274,26 @@
 
     for k in far:
         zr_copy((s + k) % ns, s).start()
+
+    tile = 128
+
+    def weights(i, _):
+        at = pl.ds(pl.multiple_of(i * tile, tile), tile)
+        x = x_all[:, at]
+        grad_gate[at, :] = dot(x, parts[:, :hid], TN).astype(BF16)
+        grad_up[at, :] = dot(x, parts[:, hid:], TN).astype(BF16)
+        return 0
+
+    lax.fori_loop(0, wg.shape[0] // tile, weights, 0)
+    stores = [
+        pltpu.make_async_copy(src, dst, out_sem.at[i])
+        for i, (src, dst) in enumerate(
+            ((grad_gate, gate_hbm), (grad_up, up_hbm), (acted, acted_hbm))
+        )
+    ]
+    for copy in stores[:2]:
+        copy.start()
+
     total = whole[s]
     for k in reversed(far):
         src = (s + k) % ns
@@ -304,9 +316,10 @@
         x_copy(expert_peer(k), e).wait_send()
     for k in range(1, ne):
         h_copy(expert_peer(k)).wait_send()
+    for k in range(1, nd):
+        p_copy((first + 1) % per * nd + (d + k) % nd).wait_send()
     for i in range(per):
         for k in range(1, nd):
-            p_copy(i * nd + (d + k) % nd).wait_send()
             o_copy((d + k) % nd, i * nd + d).wait_send()
         for side in range(2):
             a_copy(side, i * nd + d).wait_send()

time: 82.1 us -> 81.2 us (0.989)
  the two profiles are of different devices: /device:TPU:10 before, /device:TPU:24 now
where the time goes in v5:
time: 81.2 us; the launch traced here: 80 us
  Pallas kernels  79.3 us (98%)
    pallas_call x1, Pallas kernels, local(): pl.pallas_call(lambda *refs: kernel((ns, ne, nd), *refs), out_shape=(jax....  76.6 us
    pallas_call x1, Pallas kernels, local(): pl.pallas_call(settle, out_shape=tuple((jax.ShapeDtypeStruct(o.shape, o.d...  2.66 us

profile of v5, /device:TPU:24, one launch (start us, length us, event | category | flops | bytes accessed | tf_op | source)
XLA Modules:
  0.0 80.0 jit_solution(10444958837376208455)
XLA Ops:
  0.6 76.6 %shard_map.84 = (bf16[512,512]{1,0:T(8,128)(2,1)}, bf16[16,8,768]{2,1,0:T(8,128)(2,1)}, bf16[768,512]{1,0:T(8,128)(2,1)}, bf16[768,512]{1,0:T(8,128)(2,1)}) custom-call(bf16[128,768]{1,0:T(8,128)(2,1)} %refs_0_.1, s32[2,128]{1,0:T(2,128)} %bitcast.11, bf16[768,512]{1,0:T(8,128)(2,1)} %bitcast.8, bf16[768,512]{1,0:T(8,128)(2,1)} %bitcast.9, ...), custom_call_target="tpu_custom_call" | custom-call | tf_op jit(solution)/shard_map/pallas_call | solution.py:368
  77.3 2.7 %shard_map.85 = (bf16[512,512]{1,0:T(8,128)(2,1)}, bf16[16,8,768]{2,1,0:T(8,128)(2,1)}, bf16[768,512]{1,0:T(8,128)(2,1)}, bf16[768,512]{1,0:T(8,128)(2,1)}) custom-call(bf16[512,512]{1,0:T(8,128)(2,1)} %get-tuple-element.12.refs_0_, bf16[16,8,768]{2,1,0:T(8,128)(2,1)} %get-tuple-element.13.refs_1_, bf16[768,512]{1,0:T(8,128)(2,1)} %get-tuple-element.14.refs_2_, ...), custom_call_target="tpu_custom_call" | custom-call | tf_op jit(solution)/shard_map/pallas_call | solution.py:411

commit v6 on v5

--- a/solution.py
+++ b/solution.py
@@ -233,20 +233,24 @@
             back_out[rows(g), :] = back.astype(BF16)
             h_copy(g).start()
 
-    def wave(t, _):
+    def mine(t, _):
         i = (first + t) % per
         owned(i)
-
-        @pl.when(t > 0)
-        def _():
-            backward((first + t + per - 1) % per, 2)
-
-        for k in (0, 1, 3):
-            backward(i, k)
+        backward(i, 0)
         return 0
 
-    lax.fori_loop(0, per, wave, 0)
-    backward((first + per - 1) % per, 2)
+    def beside(t, _):
+        i = (first + t) % per
+        backward(i, 1)
+        backward(i, 3)
+        return 0
+
+    def opposite(t, _):
+        backward((first + t) % per, 2)
+        return 0
+
+    for step in (mine, beside, opposite):
+        lax.fori_loop(0, per, step, 0)
     for i in range(per):
         for k in range(1, nd):
             o_copy((d + k) % nd, i * nd + d).start()

time: 81.2 us -> 77.1 us (0.950)
  the two profiles are of different devices: /device:TPU:24 before, /device:TPU:4 now
where the time goes in v6:
time: 77.1 us; the launch traced here: 77 us
  Pallas kernels  76.3 us (99%)
    pallas_call x1, Pallas kernels, local(): pl.pallas_call(lambda *refs: kernel((ns, ne, nd), *refs), out_shape=(jax....  73.7 us
    pallas_call x1, Pallas kernels, local(): pl.pallas_call(settle, out_shape=tuple((jax.ShapeDtypeStruct(o.shape, o.d...  2.66 us

profile of v6, /device:TPU:4, one launch (start us, length us, event | category | flops | bytes accessed | tf_op | source)
XLA Modules:
  0.0 77.0 jit_solution(1265410428288962513)
XLA Ops:
  0.6 73.7 %shard_map.84 = (bf16[512,512]{1,0:T(8,128)(2,1)}, bf16[16,8,768]{2,1,0:T(8,128)(2,1)}, bf16[768,512]{1,0:T(8,128)(2,1)}, bf16[768,512]{1,0:T(8,128)(2,1)}) custom-call(bf16[128,768]{1,0:T(8,128)(2,1)} %refs_0_.1, s32[2,128]{1,0:T(2,128)} %bitcast.11, bf16[768,512]{1,0:T(8,128)(2,1)} %bitcast.8, bf16[768,512]{1,0:T(8,128)(2,1)} %bitcast.9, ...), custom_call_target="tpu_custom_call" | custom-call | tf_op jit(solution)/shard_map/pallas_call | solution.py:372
  74.3 2.7 %shard_map.85 = (bf16[512,512]{1,0:T(8,128)(2,1)}, bf16[16,8,768]{2,1,0:T(8,128)(2,1)}, bf16[768,512]{1,0:T(8,128)(2,1)}, bf16[768,512]{1,0:T(8,128)(2,1)}) custom-call(bf16[512,512]{1,0:T(8,128)(2,1)} %get-tuple-element.12.refs_0_, bf16[16,8,768]{2,1,0:T(8,128)(2,1)} %get-tuple-element.13.refs_1_, bf16[768,512]{1,0:T(8,128)(2,1)} %get-tuple-element.14.refs_2_, ...), custom_call_target="tpu_custom_call" | custom-call | tf_op jit(solution)/shard_map/pallas_call | solution.py:415

commit v7 on v6

--- a/solution.py
+++ b/solution.py
@@ -211,7 +211,7 @@
     def h_copy(g):
         return send(back_out.at[rows(g)], home.at[rows(e)], h_ss.at[g], h_rs.at[e], "expert", g)
 
-    def backward(i, k):
+    def arrive(i, k):
         g = i * nd + (d + k) % nd
         if k == 1:
             a_copy(0, g).wait_recv()
@@ -222,6 +222,9 @@
         elif k > 0:
             f_copy(0, g).wait_recv()
             f_copy(1, g).wait_recv()
+
+    def backward(i, k):
+        g = i * nd + (d + k) % nd
         back = dot(parts[rows(g), :hid], wg[...], NT) + dot(parts[rows(g), hid:], wu[...], NT)
 
         @pl.when(g == e)
@@ -241,11 +244,14 @@
 
     def beside(t, _):
         i = (first + t) % per
+        arrive(i, 1)
+        arrive(i, 3)
         backward(i, 1)
         backward(i, 3)
         return 0
 
     def opposite(t, _):
+        arrive((first + t) % per, 2)
         backward((first + t) % per, 2)
         return 0
 

time: 77.1 us -> 76.8 us (level)
  the two profiles are of different devices: /device:TPU:4 before, /device:TPU:22 now
where the time goes in v7:
time: 76.8 us; the launch traced here: 76.6 us
  Pallas kernels  76 us (99%)
    pallas_call x1, Pallas kernels, local(): pl.pallas_call(lambda *refs: kernel((ns, ne, nd), *refs), out_shape=(jax....  73.3 us
    pallas_call x1, Pallas kernels, local(): pl.pallas_call(settle, out_shape=tuple((jax.ShapeDtypeStruct(o.shape, o.d...  2.66 us

profile of v7, /device:TPU:22, one launch (start us, length us, event | category | flops | bytes accessed | tf_op | source)
XLA Modules:
  0.0 76.6 jit_solution(15606259937125335196)
XLA Ops:
  0.6 73.3 %shard_map.84 = (bf16[512,512]{1,0:T(8,128)(2,1)}, bf16[16,8,768]{2,1,0:T(8,128)(2,1)}, bf16[768,512]{1,0:T(8,128)(2,1)}, bf16[768,512]{1,0:T(8,128)(2,1)}) custom-call(bf16[128,768]{1,0:T(8,128)(2,1)} %refs_0_.1, s32[2,128]{1,0:T(2,128)} %bitcast.11, bf16[768,512]{1,0:T(8,128)(2,1)} %bitcast.8, bf16[768,512]{1,0:T(8,128)(2,1)} %bitcast.9, ...), custom_call_target="tpu_custom_call" | custom-call | tf_op jit(solution)/shard_map/pallas_call | solution.py:378
  74.0 2.7 %shard_map.85 = (bf16[512,512]{1,0:T(8,128)(2,1)}, bf16[16,8,768]{2,1,0:T(8,128)(2,1)}, bf16[768,512]{1,0:T(8,128)(2,1)}, bf16[768,512]{1,0:T(8,128)(2,1)}) custom-call(bf16[512,512]{1,0:T(8,128)(2,1)} %get-tuple-element.12.refs_0_, bf16[16,8,768]{2,1,0:T(8,128)(2,1)} %get-tuple-element.13.refs_1_, bf16[768,512]{1,0:T(8,128)(2,1)} %get-tuple-element.14.refs_2_, ...), custom_call_target="tpu_custom_call" | custom-call | tf_op jit(solution)/shard_map/pallas_call | solution.py:421
